TPU v7x, 32 devices: a whole 2x2x4 slice. The times are simulated.
32 devices in a mesh: groups: 2 (over y), dp: 16 (over z, x, core).
Axes of the slice: x: 2, y: 2, z: 4, core: 2. Of those that a mesh axis runs over, the one named last changes fastest.
Arguments:
- particles: bfloat16 [2048, 128, 128], P(('groups', 'dp')), parts along dimension 0, may hold values from -20 to 20
- refs: bfloat16 [128, 256, 128], P('dp', 'groups'), parts along dimension 1, may hold values from -0.5 to 0.5
- ctf_group: int32 [2048], P(('groups', 'dp')), parts along dimension 0, may hold values from 0 to 31, as said below
- defocus: float32 [64], P('groups'), parts along dimension 0, may hold values from 0.5 to 2
- class_prior: float32 [256], P('groups'), parts along dimension 0, may hold values from 0.25 to 4
- cycle_weight: float32 [64], replicated, may hold values from 0.5 to 2
Outputs:
- new_refs: float32 [128, 256, 128], P('dp', 'groups'), parts along dimension 1
- log_evidence: float32 [2048], P(('groups', 'dp')), parts along dimension 0
There are 2 independent parts, one for each index of `groups`. A program takes and returns all parts, laid end to end along the dimension named above; an argument that names none is the same for every part. Nothing has to cross between parts.
Inputs may be any that keep to these rules, and one draw needn't show every extreme that they name: `ctf_group`: CTF groups follow the particle order: particle n belongs to group n * 32 // 1024 or the next one, capped at 31.
All inputs are finite; a program needn't handle non-finite values.
Results may differ from a plain program's by a relative error of at most 0.0045.
Values may be sent and summed in bfloat16 or wider, within the bound.
A program may use at most 64 MiB of HBM per device.

v0:
```python
import math

import jax
import jax.numpy as jnp
from jax import lax
from jax.sharding import PartitionSpec as P

M = 128
R = 64
ROT = 36
G = 32


def ctf_table(defocus):
    radius = (jnp.arange(R, dtype=jnp.float32) + 1.0) / R
    phase = 20.0 * defocus[:, None] * radius[None, :] ** 2
    return -(0.995 * jnp.sin(phase) + 0.1 * jnp.cos(phase))


def angle_tables():
    harmonic = jnp.arange(M, dtype=jnp.float32)[:, None]
    turning = jnp.arange(ROT, dtype=jnp.float32)[None, :]
    theta = 2.0 * math.pi * harmonic * turning / ROT
    return (jnp.cos(theta), jnp.sin(theta))


def shards(particles, refs, ctf_group, defocus, class_prior, cycle_weight):
    highest = lax.Precision.HIGHEST
    ctf = ctf_table(defocus)
    cos_table, sin_table = angle_tables()
    onehot = (ctf_group[:, None] == jnp.arange(G, dtype=jnp.int32)[None, :]).astype(jnp.float32)
    gain_table = jnp.concatenate([cycle_weight[None, :] * ctf, cycle_weight[None, :] * ctf], axis=1)
    gain = jnp.dot(onehot, gain_table, precision=highest)
    weighted = (particles.astype(jnp.float32) * gain[:, None, :]).astype(jnp.bfloat16)
    turned = jnp.concatenate([weighted[:, :, R:], -weighted[:, :, :R]], axis=2)
    all_refs = lax.all_gather(refs, "dp", axis=0, tiled=True)
    part_weighted = weighted
    part_turned = turned
    part_cos = cos_table
    part_sin = sin_table
    cross_real = jnp.einsum(
        "nmq,mkq->mnk", part_weighted, all_refs, preferred_element_type=jnp.float32
    )
    cross_imag = jnp.einsum(
        "nmq,mkq->mnk", part_turned, all_refs, preferred_element_type=jnp.float32
    )
    corr = jnp.einsum("mnk,mj->jnk", cross_real, part_cos, precision=highest)
    corr = corr - jnp.einsum("mnk,mj->jnk", cross_imag, part_sin, precision=highest)
    wide_refs = all_refs.astype(jnp.float32)
    energy = jnp.sum(wide_refs[:, :, :R] ** 2 + wide_refs[:, :, R:] ** 2, axis=0)
    corr, energy = (corr, energy)
    quadratic = jnp.dot(cycle_weight[None, :] * ctf * ctf, energy.T, precision=highest)
    norm_term = jnp.dot(onehot, quadratic, precision=highest)
    scores = corr - 0.5 * norm_term[None, :, :] + jnp.log(class_prior)[None, None, :]
    top = jnp.max(scores, axis=(0, 2), keepdims=True)
    expo = jnp.exp(scores - top)
    total = jnp.sum(expo, axis=(0, 2), keepdims=True)
    posterior = expo / total
    log_evidence = top[0, :, 0] + jnp.log(total[0, :, 0])
    local_mass = jnp.dot(onehot.T, jnp.sum(posterior, axis=0), precision=highest)
    mass = lax.psum(local_mass, "dp")
    part_cos = cos_table
    part_sin = sin_table
    post_real = jnp.einsum("jnk,mj->mnk", posterior, part_cos, precision=highest).astype(
        jnp.bfloat16
    )
    post_imag = jnp.einsum("jnk,mj->mnk", posterior, part_sin, precision=highest).astype(
        jnp.bfloat16
    )
    part_weighted = weighted
    part_turned = turned
    term = jnp.einsum("mnk,nmq->mkq", post_real, part_weighted, preferred_element_type=jnp.float32)
    numer = lax.psum_scatter(
        term
        - jnp.einsum("mnk,nmq->mkq", post_imag, part_turned, preferred_element_type=jnp.float32),
        "dp",
        scatter_dimension=0,
        tiled=True,
    )
    denom = 1.0 + jnp.dot(mass.T, cycle_weight[None, :] * ctf * ctf, precision=highest)
    denom_wide = jnp.concatenate([denom, denom], axis=1)
    new_refs = numer / denom_wide[None, :, :]
    return (new_refs, log_evidence)


def solution(mesh):
    in_specs = (
        P(("groups", "dp"), None, None),
        P("dp", "groups", None),
        P(("groups", "dp")),
        P("groups"),
        P("groups"),
        P(),
    )
    out_specs = (P("dp", "groups", None), P(("groups", "dp")))
    return jax.shard_map(shards, mesh=mesh, in_specs=in_specs, out_specs=out_specs, check_vma=False)
```

profile of v0, /device:TPU:0, one launch (start us, length us, event | category | flops | bytes accessed | tf_op | source)
XLA Modules:
  0.0 214.6 jit_solution(5967293046546979658)
XLA Ops:
  7.2 0.0 all-gather.2.cloned.1.call-start
  7.2 0.7 all-gather.2.cloned.1.call-update
  7.9 0.0 reduce-scatter.2.cloned.1.call-start
  7.9 0.7 log.6
  8.6 0.7 broadcast_multiply_fusion
  9.3 0.8 fusion.38
  10.1 0.9 fusion.20
  11.0 2.9 %multiply_convert_fusion = bf16[64,128,128]{2,0,1:T(8,128)(2,1)S(1)} fusion(bf16[64,128,128]{2,1,0:T(8,128)(2,1)} %param.6, f32[64,128]{1,0:T(8,128)S(1)} %fusion.20), kind=kLoop, calls=%fused_computation.10 | loop fusion | flops 3145728 | bytes 4227072 | tf_op jit(solution)/shard_map/convert_element_type | solution.py:34
  13.9 2.7 %fusion.70 = (bf16[64,128,64]{2,0,1:T(8,128)(2,1)}, bf16[64,128,64]{2,0,1:T(8,128)(2,1)}) fusion(bf16[64,128,128]{2,0,1:T(8,128)(2,1)S(1)} %multiply_convert_fusion), kind=kLoop, calls=%fused_computation.77 | loop fusion | flops 524288 | bytes 4194304 | tf_op jit(solution)/shard_map/slice | solution.py:35
  16.6 46.6 %all-gather.2.cloned.1.call-done = bf16[128,128,128]{2,1,0:T(8,128)(2,1)} async-done(((bf16[8,128,128]{2,1,0:T(8,128)(2,1)}), bf16[128,128,128]{2,1,0:T(8,128)(2,1)}) %all-gather.2.cloned.1.call-update) | async-done | bytes 4194320 | tf_op jit(solution)/shard_map/all_gather | solution.py:36
  63.3 3.2 %convert_element_type.18 = f32[128,128,128]{2,1,0:T(8,128)S(1)} convert(bf16[128,128,128]{2,1,0:T(8,128)(2,1)} %all-gather.2.cloned.1.call-done) | non-fusion elementwise | flops 2097152 | bytes 12582912 | tf_op jit(solution)/shard_map/convert_element_type | solution.py:49
  66.5 0.0 copy-start.3
  66.5 0.0 copy-start.4
  66.5 0.0 copy-start
  66.5 0.0 copy-start.1
  66.5 0.0 copy-start.2
  66.6 2.5 %fusion.1 = f32[128,64]{1,0:T(8,128)S(1)} fusion(f32[128,128,128]{2,1,0:T(8,128)S(1)} %convert_element_type.18), kind=kLoop, calls=%fused_computation.2 | loop fusion | flops 4186112 | bytes 8421376 | tf_op jit(solution)/shard_map/reduce_sum | solution.py:50
  69.1 0.0 copy-done.3
  69.1 0.3 fusion.54
  69.4 0.0 copy-done.4
  69.5 0.2 convolution_multiply_fusion
  69.7 0.0 copy-done
  69.7 0.0 copy-done.1
  69.7 0.3 copy-done.2
  70.0 3.0 %fusion.18 = f32[128,64,128]{2,1,0:T(8,128)S(1)} fusion(bf16[128,128,128]{2,1,0:T(8,128)(2,1)S(1)} %copy-done, bf16[64,128,64]{2,0,1:T(8,128)(2,1)S(1)} %copy-done.2, bf16[64,128,64]{2,0,1:T(8,128)(2,1)S(1)} %copy-done.1), kind=kOutput, calls=%fused_computation.23 | convolution fusion | flops 272629760 | bytes 10485760 | tf_op jit(solution)/shard_map/nmq,mkq->mnk/dot_general | solution.py:44
  73.0 4.7 %fusion.2 = f32[36,64,128]{2,0,1:T(8,128)S(1)} fusion(f32[128,64,128]{2,1,0:T(8,128)S(1)} %fusion.18, f32[128]{0:T(128)S(1)} %iota_multiply_fusion), kind=kOutput, calls=%fused_computation.6 | convolution fusion | flops 452994048 | bytes 5374464 | tf_op jit(solution)/shard_map/mnk,mj->jnk/dot_general | solution.py:48
  77.7 3.0 %fusion.72 = f32[128,64,128]{2,1,0:T(8,128)S(1)} fusion(bf16[64,128,128]{2,0,1:T(8,128)(2,1)S(1)} %multiply_convert_fusion, bf16[128,128,128]{2,1,0:T(8,128)(2,1)S(1)} %copy-done), kind=kOutput, calls=%fused_computation.79 | convolution fusion | flops 268435456 | bytes 10485760 | tf_op jit(solution)/shard_map/nmq,mkq->mnk/dot_general | solution.py:41
  80.6 5.3 %fusion.71 = (f32[64]{0:T(128)S(1)}, f32[36,64,128]{2,0,1:T(8,128)S(1)}) fusion(f32[128]{0:T(128)S(1)} %log.6, f32[64,128]{1,0:T(8,128)S(1)} %convolution_multiply_fusion, f32[36,64,128]{2,0,1:T(8,128)S(1)} %fusion.2, f32[128,64,128]{2,1,0:T(8,128)S(1)} %fusion.72, f32[128]{0:T(128)S(1)} %iota_multiply_fusion), kind=kOutput, calls=%fused_computation.78 | convolution fusion | flops 454173632 | bytes 6587648 | tf_op jit(solution)/shard_map/mnk,mj->jnk/dot_general | solution.py:47
  85.9 1.0 fusion.17
  86.9 3.9 %fusion.24 = bf16[128,64,128]{2,0,1:T(8,128)(2,1)S(1)} fusion(f32[128]{0:T(128)S(1)} %iota_multiply_fusion, f32[36,64,128]{2,0,1:T(8,128)S(1)} %get-tuple-element.5, f32[64]{0:T(128)S(1)} %fusion.17, f32[64]{0:T(128)S(1)} %get-tuple-element.4), kind=kOutput, calls=%fused_computation.34 | convolution fusion | flops 453583872 | bytes 3277824 | tf_op jit(solution)/shard_map/jnk,mj->mnk/dot_general | solution.py:64
  90.8 3.9 %fusion.21 = bf16[128,64,128]{2,0,1:T(8,128)(2,1)S(1)} fusion(f32[128]{0:T(128)S(1)} %iota_multiply_fusion, f32[36,64,128]{2,0,1:T(8,128)S(1)} %get-tuple-element.5, f32[64]{0:T(128)S(1)} %fusion.17, f32[64]{0:T(128)S(1)} %get-tuple-element.4), kind=kOutput, calls=%fused_computation.31 | convolution fusion | flops 453583872 | bytes 3277824 | tf_op jit(solution)/shard_map/jnk,mj->mnk/dot_general | solution.py:67
  94.7 2.0 fusion.6
  96.7 6.8 %convolution_subtract_fusion = f32[128,128,128]{2,1,0:T(8,128)} fusion(f32[128,128,128]{2,1,0:T(8,128)S(1)} %fusion.6, bf16[128,64,128]{2,0,1:T(8,128)(2,1)S(1)} %fusion.21, bf16[64,128,64]{2,0,1:T(8,128)(2,1)S(1)} %copy-done.2, bf16[64,128,64]{2,0,1:T(8,128)(2,1)S(1)} %copy-done.1), kind=kOutput, calls=%fused_computation.11 | convolution fusion | flops 274726912 | bytes 20971520 | tf_op jit(solution)/shard_map/mnk,nmq->mkq/dot_general | solution.py:75
  103.5 0.0 reduce-scatter.2.cloned.1.call-update
  103.5 0.4 fusion.67
  103.9 0.3 fusion.19
  104.1 61.6 %psum.7 = f32[32,128]{1,0:T(8,128)S(1)} all-reduce(f32[32,128]{1,0:T(8,128)S(1)} %fusion.19), channel_id=1, replica_groups=mesh['groups'=2,'dp'=16] {'dp'}, use_global_device_ids=true, to_apply=%region_5.0 | all-reduce | flops 4096 | bytes 32768 | tf_op jit(solution)/shard_map/psum | solution.py:61
  165.7 0.4 convolution_add_fusion
  166.2 0.1 copy.11
  166.2 0.5 log_add_fusion
  166.8 39.1 %reduce-scatter.2.cloned.1.call-done = f32[8,128,128]{2,1,0:T(8,128)} async-done(((f32[128,128,128]{2,1,0:T(8,128)}), f32[8,128,128]{2,1,0:T(8,128)}) %reduce-scatter.2.cloned.1.call-update) | async-done | bytes 524304 | tf_op jit(solution)/shard_map/reduce_scatter | solution.py:73
  205.9 1.9 broadcast_divide_fusion
  (3 shorter events, 0.0 us)
Async XLA Ops:
  7.2 56.1 %all-gather.2.cloned.1.call-start = ((), (), s32[]{:S(2)}) async-start(), calls=%async_computation.1 | async-start | bytes 4456448 | tf_op jit(solution)/shard_map/all_gather | solution.py:36
  7.9 198.0 %reduce-scatter.2.cloned.1.call-start = ((), (), s32[]{:S(2)}) async-start(), calls=%async_computation.2 | async-start | bytes 8912896 | tf_op jit(solution)/shard_map/reduce_scatter | solution.py:73
  66.5 2.6 %copy-start.3 = (f32[64]{0:T(128)S(1)}, f32[64]{0:T(128)}, u32[]{:S(2)}) copy-start(f32[64]{0:T(128)} %param.11) | copy-start | bytes 772
  66.5 2.9 %copy-start.4 = (s32[64]{0:T(128)S(1)}, s32[64]{0:T(128)}, u32[]{:S(2)}) copy-start(s32[64]{0:T(128)} %param.8) | copy-start | bytes 772
  66.5 3.1 %copy-start = (bf16[128,128,128]{2,1,0:T(8,128)(2,1)S(1)}, bf16[128,128,128]{2,1,0:T(8,128)(2,1)}, u32[]{:S(2)}) copy-start(bf16[128,128,128]{2,1,0:T(8,128)(2,1)} %all-gather.2.cloned.1.call-done) | copy-start | bytes 12582916
  66.5 3.1 %copy-start.1 = (bf16[64,128,64]{2,0,1:T(8,128)(2,1)S(1)}, bf16[64,128,64]{2,0,1:T(8,128)(2,1)}, u32[]{:S(2)}) copy-start(bf16[64,128,64]{2,0,1:T(8,128)(2,1)} %get-tuple-element.2) | copy-start | bytes 3145732
  66.5 3.5 %copy-start.2 = (bf16[64,128,64]{2,0,1:T(8,128)(2,1)S(1)}, bf16[64,128,64]{2,0,1:T(8,128)(2,1)}, u32[]{:S(2)}) copy-start(bf16[64,128,64]{2,0,1:T(8,128)(2,1)} %get-tuple-element.3) | copy-start | bytes 3145732
Sparse Core Ops, SparseCore 0:
  10.1 53.0 all-gather.1
  103.6 102.2 reduce-scatter.1
where the time goes:
time: 215 us
  waiting for transfers between devices  86.5 us (40%)
  blocking collectives  61.6 us (29%)
  matrix products  34.5 us (16%)
  other arithmetic  16.6 us (8%)
  between operations  14.2 us (7%)
    psum x1, blocking collectives, shards(): mass = lax.psum(local_mass, 'dp')  61.6 us
    all_gather x1, waiting for transfers between devices, shards(): all_refs = lax.all_gather(refs, 'dp', axis=0, tiled=True)  46.6 us
    reduce_scatter x1, waiting for transfers between devices, shards(): lax.psum_scatter(term - jnp.einsum('mnk,nmq->mkq', post_imag, part_turned...  39.1 us
    dot_general x1, matrix products, shards(): jnp.einsum('mnk,nmq->mkq', post_imag, part_turned, preferred_element_type...  6.76 us
    dot_general x1, matrix products, shards(): corr = jnp.einsum('mnk,mj->jnk', cross_real, part_cos, precision=highest)  5.3 us
    dot_general x1, matrix products, shards(): jnp.einsum('mnk,mj->jnk', cross_imag, part_sin, precision=highest)  4.69 us
  transfers between devices with their start and end apart: 2, of which 2 were waited for; matrix products, arithmetic and copies ran while one was open for 5% of the time, Pallas kernels for 0%

commit v1 on v0

v1 whole, which is shorter than its diff:
```python
import functools
import math

import jax
import jax.numpy as jnp
from jax import lax
from jax.experimental import pallas as pl
from jax.experimental.pallas import tpu as pltpu
from jax.sharding import PartitionSpec as P

R = 64
ROT = 36
HALF = ROT // 2
NC = HALF + 1
G = 32
MESH = pl.DeviceIdType.MESH
HIGHEST = lax.Precision.HIGHEST


def ctf_table(defocus):
    radius = (jnp.arange(R, dtype=jnp.float32) + 1.0) / R
    phase = 20.0 * defocus[:, None] * radius[None, :] ** 2
    return -(0.995 * jnp.sin(phase) + 0.1 * jnp.cos(phase))


def peer_order(zn):
    return sorted(range(1, zn), key=lambda o: -min(o, zn - o))


def dev(index):
    return {"dp": index}


def gather_kernel(zn, refs_ref, wt_ref, out_ref, wpart_ref, local_sem, send, recv, wsend, wrecv):
    me = lax.axis_index("dp")
    z, x, c = me // 4, (me // 2) % 2, me % 2
    flip_x = z * 4 + (1 - x) * 2 + c
    flip_c = z * 4 + x * 2 + (1 - c)
    peers = [lax.rem(z + o, zn) * 4 + x * 2 + c for o in range(1, zn)]

    barrier = pltpu.get_barrier_semaphore()
    for p in peers + [flip_x, flip_c]:
        pl.semaphore_signal(barrier, inc=1, device_id=dev(p), device_id_type=MESH)
    pl.semaphore_wait(barrier, zn + 1)

    started = []

    def push(src, block, target, slot):
        copy = pltpu.make_async_remote_copy(
            src_ref=src,
            dst_ref=out_ref.at[block],
            send_sem=send.at[slot],
            recv_sem=recv.at[slot],
            device_id=dev(target),
            device_id_type=MESH,
        )
        copy.start()
        started.append(copy)
        return copy

    x0, c0 = zn - 1, 2 * zn - 1
    keep = pltpu.make_async_copy(refs_ref, out_ref.at[me], local_sem)
    keep.start()
    zc = {}
    for o in peer_order(zn):
        zc[o] = push(refs_ref, me, lax.rem(z + o, zn) * 4 + x * 2 + c, o - 1)
    xc = [push(refs_ref, me, flip_x, x0)]
    cc = [push(refs_ref, me, flip_c, c0)]
    wcopy = pltpu.make_async_remote_copy(
        src_ref=wt_ref.at[:, 1 - c],
        dst_ref=wpart_ref,
        send_sem=wsend,
        recv_sem=wrecv,
        device_id=dev(flip_c),
        device_id_type=MESH,
    )
    wcopy.start()
    order = sorted(range(1, zn), key=lambda o: min(o, zn - o))
    for i, o in enumerate(order):
        zc[o].wait_recv()
        block = lax.rem(z + zn - o, zn) * 4 + x * 2 + c
        xc.append(push(out_ref.at[block], block, flip_x, x0 + 1 + i))
        cc.append(push(out_ref.at[block], block, flip_c, c0 + 1 + i))
    for i, o in enumerate([0] + order):
        xc[i].wait_recv()
        block = lax.rem(z + zn - o, zn) * 4 + (1 - x) * 2 + c
        cc.append(push(out_ref.at[block], block, flip_c, c0 + zn + i))
    for copy in cc:
        copy.wait_recv()
    wcopy.wait_recv()
    for copy in started:
        copy.wait_send()
    wcopy.wait_send()
    keep.wait()


def dft_even_odd(even_in, odd_in, use_cos):
    f = math.cos if use_cos else math.sin

    def one(items, j):
        total = None
        for i, v in items:
            w = f(2.0 * math.pi * ((i * j) % ROT) / ROT)
            if abs(w) < 1e-12:
                continue
            if abs(w - 1.0) < 1e-12:
                term = v
            elif abs(w + 1.0) < 1e-12:
                term = -v
            else:
                term = v * jnp.float32(w)
            total = term if total is None else total + term
        return total

    count = HALF // 2 + 1
    return [one(even_in, j) for j in range(count)], [one(odd_in, j) for j in range(count)]


def half_transform(values, use_cos):
    even = [(i, v) for i, v in values.items() if i % 2 == 0]
    odd = [(i, v) for i, v in values.items() if i % 2 == 1]
    es, os_ = dft_even_odd(even, odd, use_cos)
    zero = jnp.zeros_like(next(iter(values.values())))
    out = {}
    for j in range(HALF // 2 + 1):
        e = zero if es[j] is None else es[j]
        o = zero if os_[j] is None else os_[j]
        out[j] = e + o
        out[HALF - j] = (e - o) if use_cos else (o - e)
    return out


def estep_kernel(refs_ref, wt_ref, anorm_ref, prior_ref, hot_ref, pp_ref, ev_ref, mass_ref, cres, energy, bias, psum):
    m_all = refs_ref.shape[0]
    n = wt_ref.shape[1]
    q = wt_ref.shape[2]
    lane = lax.broadcasted_iota(jnp.int32, (n, q), 1)
    sign = jnp.where(lane < R, jnp.float32(1.0), jnp.float32(-1.0))
    energy[...] = jnp.zeros_like(energy)

    def residue(r, count):
        acc = None
        sq = None
        for t in range(count):
            m = r + ROT * t
            w = wt_ref[m]
            turned = (pltpu.roll(w.astype(jnp.float32), R, 1) * sign).astype(jnp.bfloat16)
            both = jnp.concatenate([w, turned], axis=0)
            ref = refs_ref[m]
            part = lax.dot_general(
                both, ref, (((1,), (1,)), ((), ())), preferred_element_type=jnp.float32
            )
            acc = part if acc is None else acc + part
            wide = ref.astype(jnp.float32)
            sq = wide * wide if sq is None else sq + wide * wide
        cres[r] = acc
        energy[...] += sq

    full, extra = m_all // ROT, m_all % ROT
    if extra:
        pl.loop(0, extra)(lambda r: residue(r, full + 1))
    pl.loop(extra, ROT)(lambda r: residue(r, full))

    norm = lax.dot_general(
        anorm_ref[...], energy[...], (((1,), (1,)), ((), ())),
        preferred_element_type=jnp.float32, precision=HIGHEST,
    )
    bias[...] = prior_ref[...] - norm

    rows = 16

    @pl.loop(0, n // rows)
    def _(i):
        at = pl.ds(pl.multiple_of(i * rows, rows), rows)
        at_im = pl.ds(pl.multiple_of(n + i * rows, rows), rows)
        a = {0: cres[0, at, :], HALF: cres[HALF, at, :]}
        b = {}
        for r in range(1, HALF):
            a[r] = cres[r, at, :] + cres[ROT - r, at, :]
            b[r] = cres[r, at_im, :] - cres[ROT - r, at_im, :]
        cosine = half_transform(a, True)
        sine = half_transform(b, False)
        add = bias[at, :]
        scores = {}
        for j in range(NC):
            base = cosine[j] + add
            if j in (0, HALF):
                scores[j] = base
            else:
                scores[j] = base - sine[j]
                scores[ROT - j] = base + sine[j]
        top = scores[0]
        for j in range(1, ROT):
            top = jnp.maximum(top, scores[j])
        top = jnp.max(top, axis=1, keepdims=True)
        total = None
        expo = {}
        for j in range(ROT):
            expo[j] = jnp.exp(scores[j] - top)
            total = expo[j] if total is None else total + expo[j]
        norm_total = jnp.sum(total, axis=1, keepdims=True)
        ev_ref[at, :] = jnp.broadcast_to(top + jnp.log(norm_total), (rows, 128))
        inv = 1.0 / norm_total
        psum[at, :] = total * inv
        u = {0: expo[0] * inv, HALF: expo[HALF] * inv}
        v = {}
        for j in range(1, HALF):
            u[j] = (expo[j] + expo[ROT - j]) * inv
            v[j] = (expo[j] - expo[ROT - j]) * inv
        real = half_transform(u, True)
        imag = half_transform(v, False)
        for r in range(NC):
            pp_ref[r, at, :] = real[r].astype(jnp.bfloat16)
            pp_ref[NC + r, at, :] = imag[r].astype(jnp.bfloat16)

    mass_ref[...] = lax.dot_general(
        hot_ref[...], psum[...], (((1,), (0,)), ((), ())),
        preferred_element_type=jnp.float32, precision=HIGHEST,
    )


def mstep_kernel(zn, dp, pp_ref, wt_ref, wpart_ref, mass_ref, table_ref, out_ref,
                 pbuf, pt, xsend, xrecv, acc, zsend, zrecv, mslots,
                 psend_s, psend_r, xs, xr, zs, zr, ms, mr):
    me = lax.axis_index("dp")
    z, x, c = me // 4, (me // 2) % 2, me % 2
    flip_x = z * 4 + (1 - x) * 2 + c
    flip_c = z * 4 + x * 2 + (1 - c)
    mb, k, q = out_ref.shape

    barrier = pltpu.get_barrier_semaphore()
    for o in range(1, dp):
        pl.semaphore_signal(barrier, inc=1, device_id=dev(lax.rem(me + o, dp)), device_id_type=MESH)
    pl.semaphore_wait(barrier, dp - 1)

    pcopy = pltpu.make_async_remote_copy(
        src_ref=pp_ref, dst_ref=pbuf, send_sem=psend_s, recv_sem=psend_r,
        device_id=dev(flip_c), device_id_type=MESH,
    )
    pcopy.start()
    mcopies = []
    for o in range(1, dp):
        copy = pltpu.make_async_remote_copy(
            src_ref=mass_ref, dst_ref=mslots.at[me], send_sem=ms.at[o], recv_sem=mr.at[o],
            device_id=dev(lax.rem(me + o, dp)), device_id_type=MESH,
        )
        copy.start()
        mcopies.append(copy)
    mslots[me] = mass_ref[...]
    pcopy.wait()

    @pl.loop(0, 2 * NC)
    def _(i):
        pt[i] = jnp.concatenate([pp_ref[i], pbuf[i]], axis=0).T

    lane = lax.broadcasted_iota(jnp.int32, (k, q), 1)
    mask = jnp.where(lane < R, jnp.float32(-1.0), jnp.float32(1.0))

    def numer(zx, i):
        m = (zx * 2 + c) * mb + i
        r = lax.rem(m, ROT)
        rr = jnp.minimum(r, ROT - r)
        s = jnp.where(r > HALF, -1, 1).astype(jnp.float32)
        w = jnp.concatenate([wt_ref[zx, c, i], wpart_ref[zx, i]], axis=0)
        u = jnp.dot(pt[rr], w, preferred_element_type=jnp.float32)
        v = jnp.dot(pt[NC + rr], w, preferred_element_type=jnp.float32)
        return u + pltpu.roll(v, R, 1) * (mask * s)

    order = peer_order(zn) + [0]
    xcopies = []
    for o in order:
        zz = lax.rem(z + o, zn)

        @pl.loop(0, mb)
        def _(i):
            xsend[o, i] = numer(zz * 2 + 1 - x, i).astype(jnp.bfloat16)

        copy = pltpu.make_async_remote_copy(
            src_ref=xsend.at[o], dst_ref=xrecv.at[o], send_sem=xs.at[o], recv_sem=xr.at[o],
            device_id=dev(flip_x), device_id_type=MESH,
        )
        copy.start()
        xcopies.append(copy)

    zcopies = []
    for o, xcopy in zip(order, xcopies):
        zz = lax.rem(z + o, zn)

        @pl.loop(0, mb)
        def _(i):
            acc[i] = numer(zz * 2 + x, i)

        xcopy.wait_recv()
        if o:
            @pl.loop(0, mb)
            def _(i):
                zsend[o, i] = (acc[i] + xrecv[o, i].astype(jnp.float32)).astype(jnp.bfloat16)

            copy = pltpu.make_async_remote_copy(
                src_ref=zsend.at[o], dst_ref=zrecv.at[o], send_sem=zs.at[o], recv_sem=zr.at[o],
                device_id=dev(zz * 4 + x * 2 + c), device_id_type=MESH,
            )
            copy.start()
            zcopies.append(copy)
    for copy in mcopies:
        copy.wait_recv()
    wide = mslots[...].reshape(dp * mslots.shape[1], k)
    denom = 1.0 + lax.dot_general(
        wide, table_ref[...], (((0,), (0,)), ((), ())),
        preferred_element_type=jnp.float32, precision=HIGHEST,
    )
    inv = 1.0 / denom
    for copy in zcopies:
        copy.wait_recv()

    @pl.loop(0, mb)
    def _(i):
        total = acc[i] + xrecv[0, i].astype(jnp.float32)
        for o in range(1, zn):
            total = total + zrecv[o, i].astype(jnp.float32)
        out_ref[i] = total * inv

    for copy in xcopies + zcopies + mcopies:
        copy.wait_send()


def shards(dp, particles, refs, ctf_group, defocus, class_prior, cycle_weight):
    n, m_all, q = particles.shape
    mb, k, _ = refs.shape
    zn = dp // 4
    nall = n * dp
    me = lax.axis_index("dp")
    ctf = ctf_table(defocus)
    onehot = (ctf_group[:, None] == jnp.arange(G, dtype=jnp.int32)[None, :]).astype(jnp.float32)
    gain_table = cycle_weight[None, :] * ctf
    power = gain_table * ctf
    picked = jnp.dot(onehot, jnp.concatenate([gain_table, gain_table, power, power], axis=1), precision=HIGHEST)
    gain, anorm = picked[:, :q], 0.5 * picked[:, q:]
    weighted = (particles.astype(jnp.float32) * gain[:, None, :]).astype(jnp.bfloat16)
    wt = jnp.transpose(weighted, (1, 0, 2))
    wt6 = wt.reshape(dp // 2, 2, mb, n, q)

    window = -(-((n * G) // nall + 2) // 8) * 8
    starts = jnp.arange(dp, dtype=jnp.int32) * n * G // nall
    rel = jnp.arange(window, dtype=jnp.int32)
    hot = (ctf_group[None, :] == (starts[me] + rel)[:, None]).astype(jnp.float32)
    rows = (starts[:, None] + rel[None, :]).reshape(-1)
    table = jnp.where((rows < G)[:, None], jnp.concatenate([power, power], axis=1)[jnp.minimum(rows, G - 1)], 0.0)

    vmem = pl.BlockSpec(memory_space=pltpu.VMEM)
    hbm = pl.BlockSpec(memory_space=pl.ANY)
    copies = 4 * zn - 1
    all_refs, wpart = pl.pallas_call(
        functools.partial(gather_kernel, zn),
        out_shape=(
            jax.ShapeDtypeStruct((dp, mb, k, q), jnp.bfloat16),
            jax.ShapeDtypeStruct((dp // 2, mb, n, q), jnp.bfloat16),
        ),
        in_specs=[vmem, hbm],
        out_specs=(hbm, hbm),
        scratch_shapes=[
            pltpu.SemaphoreType.DMA,
            pltpu.SemaphoreType.DMA((copies,)),
            pltpu.SemaphoreType.DMA((copies,)),
            pltpu.SemaphoreType.DMA,
            pltpu.SemaphoreType.DMA,
        ],
        compiler_params=pltpu.CompilerParams(collective_id=0, has_side_effects=True),
        name="gather",
    )(refs, wt6)

    pp, ev, mass = pl.pallas_call(
        estep_kernel,
        out_shape=(
            jax.ShapeDtypeStruct((2 * NC, n, k), jnp.bfloat16),
            jax.ShapeDtypeStruct((n, 128), jnp.float32),
            jax.ShapeDtypeStruct((window, k), jnp.float32),
        ),
        in_specs=[vmem] * 5,
        out_specs=(vmem,) * 3,
        scratch_shapes=[
            pltpu.VMEM((ROT, 2 * n, k), jnp.float32),
            pltpu.VMEM((k, q), jnp.float32),
            pltpu.VMEM((n, k), jnp.float32),
            pltpu.VMEM((n, k), jnp.float32),
        ],
        name="estep",
    )(all_refs.reshape(m_all, k, q), wt, anorm, jnp.log(class_prior)[None, :], hot)

    sem = pltpu.SemaphoreType.DMA
    new_refs = pl.pallas_call(
        functools.partial(mstep_kernel, zn, dp),
        out_shape=jax.ShapeDtypeStruct((mb, k, q), jnp.float32),
        in_specs=[vmem] * 5,
        out_specs=vmem,
        scratch_shapes=[
            pltpu.VMEM((2 * NC, n, k), jnp.bfloat16),
            pltpu.VMEM((2 * NC, k, 2 * n), jnp.bfloat16),
            pltpu.VMEM((zn, mb, k, q), jnp.bfloat16),
            pltpu.VMEM((zn, mb, k, q), jnp.bfloat16),
            pltpu.VMEM((mb, k, q), jnp.float32),
            pltpu.VMEM((zn, mb, k, q), jnp.bfloat16),
            pltpu.VMEM((zn, mb, k, q), jnp.bfloat16),
            pltpu.VMEM((dp, window, k), jnp.float32),
            sem, sem,
            sem((zn,)), sem((zn,)), sem((zn,)), sem((zn,)), sem((dp,)), sem((dp,)),
        ],
        compiler_params=pltpu.CompilerParams(collective_id=1, has_side_effects=True),
        name="mstep",
    )(pp, wt6, wpart, mass, table)
    return (new_refs, ev[:, 0])


def solution(mesh):
    in_specs = (
        P(("groups", "dp"), None, None),
        P("dp", "groups", None),
        P(("groups", "dp")),
        P("groups"),
        P("groups"),
        P(),
    )
    out_specs = (P("dp", "groups", None), P(("groups", "dp")))
    return jax.shard_map(
        functools.partial(shards, mesh.shape["dp"]),
        mesh=mesh, in_specs=in_specs, out_specs=out_specs, check_vma=False,
    )
```

time: 215 us -> 126 us (0.59)
  Pallas kernels: 0 us -> 108 us
  waiting for transfers between devices: 86.5 us -> 0 us
  blocking collectives: 61.6 us -> 0 us
  matrix products: 34.5 us -> 0.9 us
  between operations: 14.2 us -> 0.72 us
  other arithmetic: 16.6 us -> 12 us
  local copies, waits for them, and re-layouts: 1.12 us -> 4.45 us
    pallas_call x0 -> x3, Pallas kernels: none -> 108 us  [the longest x1 53.7 us: shards(): pl.pallas_call(functools.partial(mstep_kernel, zn, dp), out_shape=jax.Sha...]
    psum x1 -> x0, blocking collectives: 61.6 us -> none  [shards(): mass = lax.psum(local_mass, 'dp')]
    all_gather x1 -> x0, waiting for transfers between devices: 46.6 us -> none  [shards(): all_refs = lax.all_gather(refs, 'dp', axis=0, tiled=True)]
    reduce_scatter x1 -> x0, waiting for transfers between devices: 39.1 us -> none  [shards(): lax.psum_scatter(term - jnp.einsum('mnk,nmq->mkq', post_imag, part_turned...]
    dot_general x13 -> x1, matrix products: 34.5 us -> 0.9 us  [shards(): jnp.dot(onehot, jnp.concatenate([gain_table, gain_table, power, power], a...]
    reduce_sum x3 -> x0, other arithmetic: 3.88 us -> none  [the longest x1 2.53 us: shards(): jnp.sum(wide_refs[:, :, :R] ** 2 + wide_refs[:, :, R:] ** 2, axis=0)]
    slice x1 -> x0, other arithmetic: 2.7 us -> none  [shards(): turned = jnp.concatenate([weighted[:, :, R:], -weighted[:, :, :R]], axis=2)]
    transpose x0 -> x1, other arithmetic: none -> 2.69 us  [shards(): wt = jnp.transpose(weighted, (1, 0, 2))]
  transfers between devices with their start and end apart: 2 -> 0, of which waited for: 2 -> 0; matrix products, arithmetic and copies ran while one was open for 5% -> 0% of each run, Pallas kernels for 0% -> 0%
where the time goes in v1:
time: 126 us
  Pallas kernels  108 us (86%)
  other arithmetic  12 us (10%)
  local copies, waits for them, and re-layouts  4.45 us (4%)
    pallas_call x1, Pallas kernels, shards(): pl.pallas_call(functools.partial(mstep_kernel, zn, dp), out_shape=jax.Sha...  53.7 us
    pallas_call x1, Pallas kernels, shards(): pl.pallas_call(functools.partial(gather_kernel, zn), out_shape=(jax.Shape...  39.6 us
    pallas_call x1, Pallas kernels, shards(): pl.pallas_call(estep_kernel, out_shape=(jax.ShapeDtypeStruct((2 * NC, n,...  14.4 us
    convert_element_type x1, other arithmetic, shards(): (particles.astype(jnp.float32) * gain[:, None, :]).astype(jnp.bfloat16)  4.27 us
    transpose x1, other arithmetic, shards(): wt = jnp.transpose(weighted, (1, 0, 2))  2.69 us

profile of v1, /device:TPU:0, one launch (start us, length us, event | category | flops | bytes accessed | tf_op | source)
XLA Modules:
  0.0 125.8 jit_solution(7479828588916299647)
XLA Ops:
  0.6 0.6 dynamic_slice.3
  1.2 0.6 iota_add_fusion.1
  1.9 1.3 %compare_convert_fusion.hot_ref = f32[8,64]{1,0:T(8,128)} fusion(s32[64]{0:T(128)} %param.8, s32[8]{0:T(128)S(1)} %iota_add_fusion.1), kind=kLoop, calls=%fused_computation.28 | loop fusion | flops 1024 | bytes 2336 | tf_op jit(solution)/shard_map/convert_element_type | solution.py:346
  3.2 0.7 broadcast_multiply_fusion
  3.9 0.8 fusion.13
  4.7 0.9 fusion
  5.6 0.6 slice_multiply_fusion
  6.2 4.3 %multiply_convert_fusion = bf16[64,128,128]{2,0,1:T(8,128)(2,1)} fusion(bf16[64,128,128]{2,1,0:T(8,128)(2,1)} %param.6, f32[64,128]{1,0:T(8,128)S(1)} %get-tuple-element.13), kind=kLoop, calls=%fused_computation.1 | loop fusion | flops 3145728 | bytes 4227072 | tf_op jit(solution)/shard_map/convert_element_type | solution.py:339
  10.5 0.0 copy-start
  10.5 39.6 %gather.7 = (bf16[16,8,128,128]{3,2,1,0:T(8,128)(2,1)}, bf16[8,8,64,128]{3,2,1,0:T(8,128)(2,1)}) custom-call(bf16[8,128,128]{2,1,0:T(8,128)(2,1)} %refs_ref.1, bf16[8,2,8,64,128]{4,3,2,1,0:T(8,128)(2,1)} %bitcast.10), custom_call_target="tpu_custom_call" | custom-call | tf_op jit(solution)/shard_map/gather/pallas_call | solution.py:353
  50.1 0.0 copy-done
  50.1 0.0 copy-start.2
  50.1 2.7 %fusion.19.wt_ref = bf16[128,64,128]{2,1,0:T(8,128)(2,1)} fusion(f32[64,128]{1,0:T(8,128)S(1)} %get-tuple-element.13, bf16[64,128,128]{2,1,0:T(8,128)(2,1)S(1)} %copy-done), kind=kLoop, calls=%fused_computation.40 | loop fusion | flops 3145728 | bytes 4227072 | tf_op jit(solution)/shard_map/transpose | solution.py:340
  52.8 0.0 copy-done.2
  52.8 0.5 log_bitcast_fusion.prior_ref
  53.3 14.4 %estep.1 = (bf16[38,64,128]{2,1,0:T(8,128)(2,1)}, f32[64,128]{1,0:T(8,128)}, f32[8,128]{1,0:T(8,128)}) custom-call(bf16[128,128,128]{2,1,0:T(8,128)(2,1)} %bitcast.12, bf16[128,64,128]{2,1,0:T(8,128)(2,1)} %fusion.19.wt_ref, f32[64,128]{1,0:T(8,128)} %get-tuple-element.12.anorm_ref, f32[1,128]{1,0:T(1,128)} %log_bitcast_fusion.prior_ref, ...), custom_call_target="tpu_custom_call" | custom-call | tf_op jit(solution)/shard_map/estep/pallas_call | solution.py:372
  67.7 0.1 pad_maximum_fusion
  67.8 0.1 fusion.15
  67.9 0.1 min.18
  68.0 0.6 gather_fusion
  68.6 0.1 fusion.16
  68.7 0.1 lt.28
  68.8 0.7 broadcast_select_fusion.table_ref
  69.5 0.0 copy-start.1
  69.5 53.7 %mstep.1 = f32[8,128,128]{2,1,0:T(8,128)} custom-call(bf16[38,64,128]{2,1,0:T(8,128)(2,1)} %get-tuple-element.8.pp_ref, bf16[8,2,8,64,128]{4,3,2,1,0:T(8,128)(2,1)} %bitcast.11, bf16[8,8,64,128]{3,2,1,0:T(8,128)(2,1)} %get-tuple-element.9.wpart_ref, f32[8,128]{1,0:T(8,128)} %get-tuple-element.10.mass_ref, f32[128,128]{1,0:T(8,128)} %broadcast_select_fusion.table_ref), custom_call_target="tpu_custom_call" | custom-call | tf_op jit(solution)/shard_map/mstep/pallas_call | solution.py:391
  123.2 0.0 copy-done.1
  123.3 0.6 slice_reduce_fusion
  123.9 1.9 %copy.14 = f32[8,128,128]{2,1,0:T(8,128)} copy(f32[8,128,128]{2,1,0:T(8,128)} %mstep.1) | data formatting | bytes 1048576
  (4 shorter events, 0.0 us)
Async XLA Ops:
  10.5 39.6 %copy-start = (bf16[64,128,128]{2,1,0:T(8,128)(2,1)S(1)}, bf16[64,128,128]{2,1,0:T(8,128)(2,1)}, u32[]{:S(2)}) copy-start(bf16[64,128,128]{2,1,0:T(8,128)(2,1)} %param.6) | copy-start | bytes 6291460
  50.1 2.7 %copy-start.2 = (f32[128]{0:T(128)S(1)}, f32[128]{0:T(128)}, u32[]{:S(2)}) copy-start(f32[128]{0:T(128)} %param.10) | copy-start | bytes 1540
  69.5 53.7 %copy-start.1 = (f32[64,128]{1,0:T(8,128)S(1)}, f32[64,128]{1,0:T(8,128)}, u32[]{:S(2)}) copy-start(f32[64,128]{1,0:T(8,128)} %get-tuple-element.11) | copy-start | bytes 98308

commit v2 on v1

--- a/solution.py
+++ b/solution.py
@@ -17,31 +17,40 @@
 HIGHEST = lax.Precision.HIGHEST
 
 
-def ctf_table(defocus):
-    radius = (jnp.arange(R, dtype=jnp.float32) + 1.0) / R
-    phase = 20.0 * defocus[:, None] * radius[None, :] ** 2
-    return -(0.995 * jnp.sin(phase) + 0.1 * jnp.cos(phase))
-
-
-def peer_order(zn):
-    return sorted(range(1, zn), key=lambda o: -min(o, zn - o))
-
-
 def dev(index):
     return {"dp": index}
 
 
-def gather_kernel(zn, refs_ref, wt_ref, out_ref, wpart_ref, local_sem, send, recv, wsend, wrecv):
+def ring_steps(zn):
+    plus = zn // 2
+    minus = zn - 1 - plus
+    steps = []
+    for d in range(1, plus + 1):
+        steps.append((1, d))
+        if d <= minus:
+            steps.append((-1, d))
+    return steps
+
+
+def gather_kernel(zn, dp, window, refs_ref, part_ref, col_ref, row_ref, focus_ref, cw_ref,
+                  out_ref, wt_ref, wpart_ref, anorm_ref, hot_ref, table_ref,
+                  local_sem, send, recv, wsend, wrecv):
     me = lax.axis_index("dp")
     z, x, c = me // 4, (me // 2) % 2, me % 2
     flip_x = z * 4 + (1 - x) * 2 + c
     flip_c = z * 4 + x * 2 + (1 - c)
-    peers = [lax.rem(z + o, zn) * 4 + x * 2 + c for o in range(1, zn)]
+    steps = ring_steps(zn)
+    reach = {1: zn // 2, -1: zn - 1 - zn // 2}
+    beside = {s: lax.rem(z + zn + s, zn) * 4 + x * 2 + c for s in {d for d, _ in steps}}
+    n, m_all, q = part_ref.shape
+    mb = refs_ref.shape[0]
+    nall = n * dp
 
     barrier = pltpu.get_barrier_semaphore()
-    for p in peers + [flip_x, flip_c]:
+    greet = list(beside.values()) + [flip_x, flip_c]
+    for p in greet:
         pl.semaphore_signal(barrier, inc=1, device_id=dev(p), device_id_type=MESH)
-    pl.semaphore_wait(barrier, zn + 1)
+    pl.semaphore_wait(barrier, len(greet))
 
     started = []
 
@@ -59,38 +68,74 @@
         return copy
 
     x0, c0 = zn - 1, 2 * zn - 1
+    slot_of = {step: i for i, step in enumerate(steps)}
+    zc = {}
+    for s in beside:
+        zc[(s, 1)] = push(refs_ref, me, beside[s], slot_of[(s, 1)])
+    xc = [push(refs_ref, me, flip_x, x0)]
+    cc = [push(refs_ref, me, flip_c, c0)]
     keep = pltpu.make_async_copy(refs_ref, out_ref.at[me], local_sem)
     keep.start()
-    zc = {}
-    for o in peer_order(zn):
-        zc[o] = push(refs_ref, me, lax.rem(z + o, zn) * 4 + x * 2 + c, o - 1)
-    xc = [push(refs_ref, me, flip_x, x0)]
-    cc = [push(refs_ref, me, flip_c, c0)]
-    wcopy = pltpu.make_async_remote_copy(
-        src_ref=wt_ref.at[:, 1 - c],
-        dst_ref=wpart_ref,
-        send_sem=wsend,
-        recv_sem=wrecv,
-        device_id=dev(flip_c),
-        device_id_type=MESH,
-    )
-    wcopy.start()
-    order = sorted(range(1, zn), key=lambda o: min(o, zn - o))
-    for i, o in enumerate(order):
-        zc[o].wait_recv()
-        block = lax.rem(z + zn - o, zn) * 4 + x * 2 + c
+
+    lane = lax.broadcasted_iota(jnp.int32, (G, q), 1)
+    radius = (jnp.where(lane < R, lane, lane - R).astype(jnp.float32) + 1.0) / R
+    phase = 20.0 * focus_ref[...] * (radius * radius)
+    ctf = -(0.995 * jnp.sin(phase) + 0.1 * jnp.cos(phase))
+    cw = jnp.concatenate([cw_ref[...], cw_ref[...]], axis=1)
+    gain_table = cw * ctf
+    power = gain_table * ctf
+
+    def dot(a, b):
+        return jnp.dot(a, b, precision=HIGHEST, preferred_element_type=jnp.float32)
+
+    onehot = (col_ref[...] == lax.broadcasted_iota(jnp.int32, (n, G), 1)).astype(jnp.float32)
+    gain = dot(onehot, gain_table)
+    anorm_ref[...] = 0.5 * dot(onehot, power)
+    start = (me * (n * G)) // nall
+    hot_ref[...] = (
+        row_ref[...] == lax.broadcasted_iota(jnp.int32, (window, n), 0) + start
+    ).astype(jnp.float32)
+    below = lax.broadcasted_iota(jnp.int32, (window, G), 0) - lax.broadcasted_iota(jnp.int32, (window, G), 1)
+    for d in range(dp):
+        pick = (below == -(d * n * G // nall)).astype(jnp.float32)
+        table_ref[d * window:(d + 1) * window, :] = dot(pick, power)
+
+    chunk = 16
+
+    @pl.loop(0, m_all // chunk)
+    def _(i):
+        at = pl.ds(pl.multiple_of(i * chunk, chunk), chunk)
+        wide = part_ref[:, at, :].astype(jnp.float32) * gain[:, None, :]
+        wt_ref[at] = jnp.swapaxes(wide, 0, 1).astype(jnp.bfloat16)
+
+    for i, (s, d) in enumerate(steps):
+        zc[(s, d)].wait_recv()
+        block = lax.rem(z + zn - s * d, zn) * 4 + x * 2 + c
+        if d < reach[s]:
+            zc[(s, d + 1)] = push(out_ref.at[block], block, beside[s], slot_of[(s, d + 1)])
         xc.append(push(out_ref.at[block], block, flip_x, x0 + 1 + i))
         cc.append(push(out_ref.at[block], block, flip_c, c0 + 1 + i))
-    for i, o in enumerate([0] + order):
+        if i == 0:
+            wcopies = []
+            for b in range(dp // 2):
+                copy = pltpu.make_async_remote_copy(
+                    src_ref=wt_ref.at[pl.ds((2 * b + 1 - c) * mb, mb)],
+                    dst_ref=wpart_ref.at[b],
+                    send_sem=wsend.at[b],
+                    recv_sem=wrecv.at[b],
+                    device_id=dev(flip_c),
+                    device_id_type=MESH,
+                )
+                copy.start()
+                wcopies.append(copy)
+    for i, (s, d) in enumerate([(1, 0)] + steps):
         xc[i].wait_recv()
-        block = lax.rem(z + zn - o, zn) * 4 + (1 - x) * 2 + c
+        block = lax.rem(z + zn - s * d, zn) * 4 + (1 - x) * 2 + c
         cc.append(push(out_ref.at[block], block, flip_c, c0 + zn + i))
-    for copy in cc:
+    for copy in cc + wcopies:
         copy.wait_recv()
-    wcopy.wait_recv()
-    for copy in started:
+    for copy in started + wcopies:
         copy.wait_send()
-    wcopy.wait_send()
     keep.wait()
 
 
@@ -165,7 +210,7 @@
         anorm_ref[...], energy[...], (((1,), (1,)), ((), ())),
         preferred_element_type=jnp.float32, precision=HIGHEST,
     )
-    bias[...] = prior_ref[...] - norm
+    bias[...] = jnp.log(prior_ref[...]) - norm
 
     rows = 16
 
@@ -261,14 +306,16 @@
         r = lax.rem(m, ROT)
         rr = jnp.minimum(r, ROT - r)
         s = jnp.where(r > HALF, -1, 1).astype(jnp.float32)
-        w = jnp.concatenate([wt_ref[zx, c, i], wpart_ref[zx, i]], axis=0)
+        w = jnp.concatenate([wt_ref[m], wpart_ref[zx, i]], axis=0)
         u = jnp.dot(pt[rr], w, preferred_element_type=jnp.float32)
         v = jnp.dot(pt[NC + rr], w, preferred_element_type=jnp.float32)
         return u + pltpu.roll(v, R, 1) * (mask * s)
 
-    order = peer_order(zn) + [0]
+    steps = ring_steps(zn)
+    reach = {1: zn // 2, -1: zn - 1 - zn // 2}
+    order = [((s * (reach[s] + 1 - d)) % zn, s, d) for s, d in steps] + [(0, 0, 0)]
     xcopies = []
-    for o in order:
+    for o, _, _ in order:
         zz = lax.rem(z + o, zn)
 
         @pl.loop(0, mb)
@@ -282,8 +329,9 @@
         copy.start()
         xcopies.append(copy)
 
-    zcopies = []
-    for o, xcopy in zip(order, xcopies):
+    zcopies = {}
+    last = []
+    for j, ((o, s, d), xcopy) in enumerate(zip(order, xcopies)):
         zz = lax.rem(z + o, zn)
 
         @pl.loop(0, mb)
@@ -292,16 +340,26 @@
 
         xcopy.wait_recv()
         if o:
+            before = None
+            if d > 1:
+                before, got = zcopies[(s, d - 1)]
+                got.wait_recv()
+
             @pl.loop(0, mb)
             def _(i):
-                zsend[o, i] = (acc[i] + xrecv[o, i].astype(jnp.float32)).astype(jnp.bfloat16)
+                total = acc[i] + xrecv[o, i].astype(jnp.float32)
+                if before is not None:
+                    total = total + zrecv[before, i].astype(jnp.float32)
+                zsend[j, i] = total.astype(jnp.bfloat16)
 
             copy = pltpu.make_async_remote_copy(
-                src_ref=zsend.at[o], dst_ref=zrecv.at[o], send_sem=zs.at[o], recv_sem=zr.at[o],
-                device_id=dev(zz * 4 + x * 2 + c), device_id_type=MESH,
+                src_ref=zsend.at[j], dst_ref=zrecv.at[j], send_sem=zs.at[j], recv_sem=zr.at[j],
+                device_id=dev(lax.rem(z + zn + s, zn) * 4 + x * 2 + c), device_id_type=MESH,
             )
             copy.start()
-            zcopies.append(copy)
+            zcopies[(s, d)] = (j, copy)
+            if d == reach[s]:
+                last.append((j, copy))
     for copy in mcopies:
         copy.wait_recv()
     wide = mslots[...].reshape(dp * mslots.shape[1], k)
@@ -310,17 +368,17 @@
         preferred_element_type=jnp.float32, precision=HIGHEST,
     )
     inv = 1.0 / denom
-    for copy in zcopies:
+    for _, copy in last:
         copy.wait_recv()
 
     @pl.loop(0, mb)
     def _(i):
         total = acc[i] + xrecv[0, i].astype(jnp.float32)
-        for o in range(1, zn):
-            total = total + zrecv[o, i].astype(jnp.float32)
+        for j, _ in last:
+            total = total + zrecv[j, i].astype(jnp.float32)
         out_ref[i] = total * inv
 
-    for copy in xcopies + zcopies + mcopies:
+    for copy in xcopies + [copy for _, copy in zcopies.values()] + mcopies:
         copy.wait_send()
 
 
@@ -329,45 +387,30 @@
     mb, k, _ = refs.shape
     zn = dp // 4
     nall = n * dp
-    me = lax.axis_index("dp")
-    ctf = ctf_table(defocus)
-    onehot = (ctf_group[:, None] == jnp.arange(G, dtype=jnp.int32)[None, :]).astype(jnp.float32)
-    gain_table = cycle_weight[None, :] * ctf
-    power = gain_table * ctf
-    picked = jnp.dot(onehot, jnp.concatenate([gain_table, gain_table, power, power], axis=1), precision=HIGHEST)
-    gain, anorm = picked[:, :q], 0.5 * picked[:, q:]
-    weighted = (particles.astype(jnp.float32) * gain[:, None, :]).astype(jnp.bfloat16)
-    wt = jnp.transpose(weighted, (1, 0, 2))
-    wt6 = wt.reshape(dp // 2, 2, mb, n, q)
-
     window = -(-((n * G) // nall + 2) // 8) * 8
-    starts = jnp.arange(dp, dtype=jnp.int32) * n * G // nall
-    rel = jnp.arange(window, dtype=jnp.int32)
-    hot = (ctf_group[None, :] == (starts[me] + rel)[:, None]).astype(jnp.float32)
-    rows = (starts[:, None] + rel[None, :]).reshape(-1)
-    table = jnp.where((rows < G)[:, None], jnp.concatenate([power, power], axis=1)[jnp.minimum(rows, G - 1)], 0.0)
 
     vmem = pl.BlockSpec(memory_space=pltpu.VMEM)
     hbm = pl.BlockSpec(memory_space=pl.ANY)
     copies = 4 * zn - 1
-    all_refs, wpart = pl.pallas_call(
-        functools.partial(gather_kernel, zn),
+    sem = pltpu.SemaphoreType.DMA
+    all_refs, wt, wpart, anorm, hot, table = pl.pallas_call(
+        functools.partial(gather_kernel, zn, dp, window),
         out_shape=(
             jax.ShapeDtypeStruct((dp, mb, k, q), jnp.bfloat16),
+            jax.ShapeDtypeStruct((m_all, n, q), jnp.bfloat16),
             jax.ShapeDtypeStruct((dp // 2, mb, n, q), jnp.bfloat16),
+            jax.ShapeDtypeStruct((n, q), jnp.float32),
+            jax.ShapeDtypeStruct((window, n), jnp.float32),
+            jax.ShapeDtypeStruct((dp * window, q), jnp.float32),
         ),
-        in_specs=[vmem, hbm],
-        out_specs=(hbm, hbm),
+        in_specs=[vmem] * 6,
+        out_specs=(hbm, vmem, hbm, vmem, vmem, vmem),
         scratch_shapes=[
-            pltpu.SemaphoreType.DMA,
-            pltpu.SemaphoreType.DMA((copies,)),
-            pltpu.SemaphoreType.DMA((copies,)),
-            pltpu.SemaphoreType.DMA,
-            pltpu.SemaphoreType.DMA,
+            sem, sem((copies,)), sem((copies,)), sem((dp // 2,)), sem((dp // 2,)),
         ],
         compiler_params=pltpu.CompilerParams(collective_id=0, has_side_effects=True),
         name="gather",
-    )(refs, wt6)
+    )(refs, particles, ctf_group[:, None], ctf_group[None, :], defocus[:, None], cycle_weight[None, :])
 
     pp, ev, mass = pl.pallas_call(
         estep_kernel,
@@ -385,9 +428,8 @@
             pltpu.VMEM((n, k), jnp.float32),
         ],
         name="estep",
-    )(all_refs.reshape(m_all, k, q), wt, anorm, jnp.log(class_prior)[None, :], hot)
-
-    sem = pltpu.SemaphoreType.DMA
+    )(all_refs.reshape(m_all, k, q), wt, anorm, class_prior[None, :], hot)
+
     new_refs = pl.pallas_call(
         functools.partial(mstep_kernel, zn, dp),
         out_shape=jax.ShapeDtypeStruct((mb, k, q), jnp.float32),
@@ -407,7 +449,7 @@
         ],
         compiler_params=pltpu.CompilerParams(collective_id=1, has_side_effects=True),
         name="mstep",
-    )(pp, wt6, wpart, mass, table)
+    )(pp, wt, wpart, mass, table)
     return (new_refs, ev[:, 0])
 
 

time: 126 us -> 95.9 us (0.76)
  Pallas kernels: 108 us -> 89.8 us
  other arithmetic: 12 us -> 0 us
    pallas_call x1, Pallas kernels: 53.7 us -> 39.4 us  [shards(): pl.pallas_call(functools.partial(mstep_kernel, zn, dp), out_shape=jax.Sha...]
    convert_element_type x2 -> x0, other arithmetic: 5.58 us -> none  [the longest x1 4.27 us: shards(): (particles.astype(jnp.float32) * gain[:, None, :]).astype(jnp.bfloat16)]
    pallas_call x1, Pallas kernels: 39.6 us -> 36 us  [shards(): pl.pallas_call(functools.partial(gather_kernel, zn, dp, window), out_shap...]
    transpose x1 -> x0, other arithmetic: 2.69 us -> none  [shards(): wt = jnp.transpose(weighted, (1, 0, 2))]
    broadcast_in_dim x1 -> x2, local copies, waits for them, and re-layouts: 0.52 us -> 2.69 us  [the longest x1 1.36 us: shards(): ctf_group[:, None]]
    mul x3 -> x0, other arithmetic: 2.08 us -> none  [the longest x1 0.8 us: shards(): gain_table = cycle_weight[None, :] * ctf]
where the time goes in v2:
time: 95.9 us; the launch traced here: 95.6 us
  Pallas kernels  89.8 us (94%)
  local copies, waits for them, and re-layouts  5.19 us (5%)
    pallas_call x1, Pallas kernels, shards(): pl.pallas_call(functools.partial(mstep_kernel, zn, dp), out_shape=jax.Sha...  39.4 us
    pallas_call x1, Pallas kernels, shards(): pl.pallas_call(functools.partial(gather_kernel, zn, dp, window), out_shap...  36 us
    pallas_call x1, Pallas kernels, shards(): pl.pallas_call(estep_kernel, out_shape=(jax.ShapeDtypeStruct((2 * NC, n,...  14.4 us

profile of v2, /device:TPU:0, one launch (start us, length us, event | category | flops | bytes accessed | tf_op | source)
XLA Modules:
  0.0 95.6 jit_solution(9965400897073484679)
XLA Ops:
  0.6 1.3 %copy.11.focus_ref = f32[32,1]{1,0:T(8,128)} copy(f32[32,1]{0,1:T(1,128)} %bitcast.11) | data formatting | bytes 256 | tf_op jit(solution)/shard_map/broadcast_in_dim | solution.py:413
  2.0 1.4 %copy.10.col_ref = s32[64,1]{1,0:T(8,128)} copy(s32[64,1]{0,1:T(1,128)} %bitcast.7) | data formatting | bytes 512 | tf_op jit(solution)/shard_map/broadcast_in_dim | solution.py:413
  3.3 36.0 %gather.1 = (bf16[16,8,128,128]{3,2,1,0:T(8,128)(2,1)}, bf16[128,64,128]{2,1,0:T(8,128)(2,1)}, bf16[8,8,64,128]{3,2,1,0:T(8,128)(2,1)}, f32[64,128]{1,0:T(8,128)}, f32[8,64]{1,0:T(8,128)}, /*index=5*/f32[128,128]{1,0:T(8,128)}) custom-call(bf16[8,128,128]{2,1,0:T(8,128)(2,1)} %refs_ref.1, bf16[64,128,128]{2,1,0:T(8,128)(2,1)} %part_ref.1, ...), custom_call_target="tpu_custom_call" | custom-call | tf_op jit(solution)/shard_map/gather/pallas_call | solution.py:396
  39.4 14.4 %estep.1 = (bf16[38,64,128]{2,1,0:T(8,128)(2,1)}, f32[64,128]{1,0:T(8,128)}, f32[8,128]{1,0:T(8,128)}) custom-call(bf16[128,128,128]{2,1,0:T(8,128)(2,1)} %bitcast.6, bf16[128,64,128]{2,1,0:T(8,128)(2,1)} %get-tuple-element.12.wt_ref, f32[64,128]{1,0:T(8,128)} %get-tuple-element.13.anorm_ref, f32[1,128]{1,0:T(1,128)} %bitcast.10, ...), custom_call_target="tpu_custom_call" | custom-call | tf_op jit(solution)/shard_map/estep/pallas_call | solution.py:415
  53.7 0.0 copy-start
  53.7 39.4 %mstep.1 = f32[8,128,128]{2,1,0:T(8,128)} custom-call(bf16[38,64,128]{2,1,0:T(8,128)(2,1)} %get-tuple-element.15.pp_ref, bf16[128,64,128]{2,1,0:T(8,128)(2,1)} %get-tuple-element.12.wt_ref, bf16[8,8,64,128]{3,2,1,0:T(8,128)(2,1)} %get-tuple-element.16.wpart_ref, f32[8,128]{1,0:T(8,128)} %get-tuple-element.17.mass_ref, f32[128,128]{1,0:T(8,128)} %get-tuple-element.18.table_ref), custom_call_target="tpu_custom_call" | custom-call | tf_op jit(solution)/shard_map/mstep/pallas_call | solution.py:433
  93.1 0.0 copy-done
  93.1 0.6 slice_reduce_fusion
  93.8 1.9 %copy.13 = f32[8,128,128]{2,1,0:T(8,128)} copy(f32[8,128,128]{2,1,0:T(8,128)} %mstep.1) | data formatting | bytes 1048576
Async XLA Ops:
  53.7 39.4 %copy-start = (f32[64,128]{1,0:T(8,128)S(1)}, f32[64,128]{1,0:T(8,128)}, u32[]{:S(2)}) copy-start(f32[64,128]{1,0:T(8,128)} %get-tuple-element.19) | copy-start | bytes 98308

commit v3 on v2

--- a/solution.py
+++ b/solution.py
@@ -32,30 +32,39 @@
     return steps
 
 
-def gather_kernel(zn, dp, window, refs_ref, part_ref, col_ref, row_ref, focus_ref, cw_ref,
-                  out_ref, wt_ref, wpart_ref, anorm_ref, hot_ref, table_ref,
-                  local_sem, send, recv, wsend, wrecv):
+def gather_kernel(zn, dp, window, refs_ref, part_ref, row_ref, focus_ref, cw_ref, prior_ref,
+                  wt_ref, wpart_ref, table_ref, pp_ref, ev_ref, mass_ref,
+                  out_ref, cres, energy, bias, psum, evcol, local_sem, send, recv, wsend, wrecv):
     me = lax.axis_index("dp")
     z, x, c = me // 4, (me // 2) % 2, me % 2
     flip_x = z * 4 + (1 - x) * 2 + c
     flip_c = z * 4 + x * 2 + (1 - c)
-    steps = ring_steps(zn)
-    reach = {1: zn // 2, -1: zn - 1 - zn // 2}
-    beside = {s: lax.rem(z + zn + s, zn) * 4 + x * 2 + c for s in {d for d, _ in steps}}
     n, m_all, q = part_ref.shape
-    mb = refs_ref.shape[0]
+    mb, k, _ = refs_ref.shape
     nall = n * dp
+    steps = [(s, d) for d in range(1, zn) for s in (1, -1)]
+    beside = {s: lax.rem(z + zn + s, zn) * 4 + x * 2 + c for s in (1, -1)}
+
+    def holds(s, d):
+        return z >= d if s == 1 else z + d < zn
+
+    def goes(s):
+        return z + 1 < zn if s == 1 else z >= 1
+
+    def origin(s, d):
+        return lax.rem(z + zn - s * d, zn) * 4
 
     barrier = pltpu.get_barrier_semaphore()
-    greet = list(beside.values()) + [flip_x, flip_c]
+    greet = [beside[1], beside[-1], flip_x, flip_c]
     for p in greet:
         pl.semaphore_signal(barrier, inc=1, device_id=dev(p), device_id_type=MESH)
     pl.semaphore_wait(barrier, len(greet))
 
-    started = []
-
-    def push(src, block, target, slot):
-        copy = pltpu.make_async_remote_copy(
+    count = 2 * (zn - 1)
+    x0, c0 = count, 2 * count + 1
+
+    def copy_of(src, block, target, slot):
+        return pltpu.make_async_remote_copy(
             src_ref=src,
             dst_ref=out_ref.at[block],
             send_sem=send.at[slot],
@@ -63,23 +72,22 @@
             device_id=dev(target),
             device_id_type=MESH,
         )
-        copy.start()
-        started.append(copy)
-        return copy
-
-    x0, c0 = zn - 1, 2 * zn - 1
+
     slot_of = {step: i for i, step in enumerate(steps)}
-    zc = {}
-    for s in beside:
-        zc[(s, 1)] = push(refs_ref, me, beside[s], slot_of[(s, 1)])
-    xc = [push(refs_ref, me, flip_x, x0)]
-    cc = [push(refs_ref, me, flip_c, c0)]
+    for s in (1, -1):
+        @pl.when(goes(s))
+        def _():
+            copy_of(refs_ref, me, beside[s], slot_of[(s, 1)]).start()
+    copy_of(refs_ref, me, flip_x, x0).start()
+    copy_of(refs_ref, me, flip_c, c0).start()
     keep = pltpu.make_async_copy(refs_ref, out_ref.at[me], local_sem)
     keep.start()
 
     lane = lax.broadcasted_iota(jnp.int32, (G, q), 1)
     radius = (jnp.where(lane < R, lane, lane - R).astype(jnp.float32) + 1.0) / R
-    phase = 20.0 * focus_ref[...] * (radius * radius)
+    eye = lax.broadcasted_iota(jnp.int32, (G, G), 0) == lax.broadcasted_iota(jnp.int32, (G, G), 1)
+    focus = jnp.sum(jnp.where(eye, jnp.broadcast_to(focus_ref[...], (G, G)), 0.0), axis=1, keepdims=True)
+    phase = 20.0 * focus * (radius * radius)
     ctf = -(0.995 * jnp.sin(phase) + 0.1 * jnp.cos(phase))
     cw = jnp.concatenate([cw_ref[...], cw_ref[...]], axis=1)
     gain_table = cw * ctf
@@ -88,11 +96,18 @@
     def dot(a, b):
         return jnp.dot(a, b, precision=HIGHEST, preferred_element_type=jnp.float32)
 
-    onehot = (col_ref[...] == lax.broadcasted_iota(jnp.int32, (n, G), 1)).astype(jnp.float32)
-    gain = dot(onehot, gain_table)
-    anorm_ref[...] = 0.5 * dot(onehot, power)
+    onehot = (row_ref[...] == lax.broadcasted_iota(jnp.int32, (G, n), 0)).astype(jnp.float32)
+
+    def picked(table):
+        return lax.dot_general(
+            onehot, table, (((0,), (0,)), ((), ())),
+            preferred_element_type=jnp.float32, precision=HIGHEST,
+        )
+
+    gain = picked(gain_table)
+    anorm = 0.5 * picked(power)
     start = (me * (n * G)) // nall
-    hot_ref[...] = (
+    hot = (
         row_ref[...] == lax.broadcasted_iota(jnp.int32, (window, n), 0) + start
     ).astype(jnp.float32)
     below = lax.broadcasted_iota(jnp.int32, (window, G), 0) - lax.broadcasted_iota(jnp.int32, (window, G), 1)
@@ -108,35 +123,107 @@
         wide = part_ref[:, at, :].astype(jnp.float32) * gain[:, None, :]
         wt_ref[at] = jnp.swapaxes(wide, 0, 1).astype(jnp.bfloat16)
 
+    wcopies = []
+    for b in range(dp // 2):
+        copy = pltpu.make_async_remote_copy(
+            src_ref=wt_ref.at[pl.ds((2 * b + 1 - c) * mb, mb)],
+            dst_ref=wpart_ref.at[b],
+            send_sem=wsend.at[b],
+            recv_sem=wrecv.at[b],
+            device_id=dev(flip_c),
+            device_id_type=MESH,
+        )
+        copy.start()
+        wcopies.append(copy)
+
+    cres[...] = jnp.zeros_like(cres)
+    energy[...] = jnp.zeros_like(energy)
+    lane_n = lax.broadcasted_iota(jnp.int32, (n, q), 1)
+    sign = jnp.where(lane_n < R, jnp.float32(1.0), jnp.float32(-1.0))
+
+    def products(block):
+        @pl.loop(0, mb)
+        def _(i):
+            m = block * mb + i
+            r = lax.rem(m, ROT)
+            w = wt_ref[m]
+            turned = (pltpu.roll(w.astype(jnp.float32), R, 1) * sign).astype(jnp.bfloat16)
+            both = jnp.concatenate([w, turned], axis=0)
+            ref = out_ref[block, i]
+            cres[r] += lax.dot_general(
+                both, ref, (((1,), (1,)), ((), ())), preferred_element_type=jnp.float32
+            )
+            wide = ref.astype(jnp.float32)
+            energy[...] += wide * wide
+
+    keep.wait()
+    products(me)
     for i, (s, d) in enumerate(steps):
-        zc[(s, d)].wait_recv()
-        block = lax.rem(z + zn - s * d, zn) * 4 + x * 2 + c
-        if d < reach[s]:
-            zc[(s, d + 1)] = push(out_ref.at[block], block, beside[s], slot_of[(s, d + 1)])
-        xc.append(push(out_ref.at[block], block, flip_x, x0 + 1 + i))
-        cc.append(push(out_ref.at[block], block, flip_c, c0 + 1 + i))
-        if i == 0:
-            wcopies = []
-            for b in range(dp // 2):
-                copy = pltpu.make_async_remote_copy(
-                    src_ref=wt_ref.at[pl.ds((2 * b + 1 - c) * mb, mb)],
-                    dst_ref=wpart_ref.at[b],
-                    send_sem=wsend.at[b],
-                    recv_sem=wrecv.at[b],
-                    device_id=dev(flip_c),
-                    device_id_type=MESH,
-                )
-                copy.start()
-                wcopies.append(copy)
-    for i, (s, d) in enumerate([(1, 0)] + steps):
-        xc[i].wait_recv()
-        block = lax.rem(z + zn - s * d, zn) * 4 + (1 - x) * 2 + c
-        cc.append(push(out_ref.at[block], block, flip_c, c0 + zn + i))
-    for copy in cc + wcopies:
-        copy.wait_recv()
-    for copy in started + wcopies:
-        copy.wait_send()
-    keep.wait()
+        @pl.when(holds(s, d))
+        def _():
+            block = origin(s, d) + x * 2 + c
+            copy_of(out_ref.at[block], block, beside[s], slot_of[(s, d)]).wait_recv()
+            if d + 1 < zn:
+                @pl.when(goes(s))
+                def _():
+                    copy_of(out_ref.at[block], block, beside[s], slot_of[(s, d + 1)]).start()
+            copy_of(out_ref.at[block], block, flip_x, x0 + 1 + i).start()
+            copy_of(out_ref.at[block], block, flip_c, c0 + 1 + i).start()
+            products(block)
+    every = [(None, (1, 0))] + list(enumerate(steps))
+
+    def guarded(s, d, body):
+        if d == 0:
+            body()
+        else:
+            pl.when(holds(s, d))(body)
+
+    for i, (s, d) in every:
+        j = 0 if i is None else i + 1
+
+        def from_x(s=s, d=d, j=j):
+            block = origin(s, d) + (1 - x) * 2 + c
+            copy_of(out_ref.at[block], block, flip_x, x0 + j).wait_recv()
+            copy_of(out_ref.at[block], block, flip_c, c0 + count + 1 + j).start()
+            products(block)
+            mine = origin(s, d) + x * 2 + (1 - c)
+            copy_of(out_ref.at[mine], mine, flip_c, c0 + j).wait_recv()
+            products(mine)
+
+        guarded(s, d, from_x)
+    for i, (s, d) in every:
+        j = 0 if i is None else i + 1
+
+        def from_core(s=s, d=d, j=j):
+            block = origin(s, d) + (1 - x) * 2 + (1 - c)
+            copy_of(out_ref.at[block], block, flip_c, c0 + count + 1 + j).wait_recv()
+            products(block)
+
+        guarded(s, d, from_core)
+
+    scores_and_posterior(anorm, hot, prior_ref, pp_ref, ev_ref, mass_ref, cres, energy, bias, psum, evcol, n)
+
+    for copy in wcopies:
+        copy.wait()
+    for i, (s, d) in every:
+        j = 0 if i is None else i + 1
+
+        def sent(s=s, d=d, j=j):
+            block = origin(s, d) + x * 2 + c
+            other = origin(s, d) + (1 - x) * 2 + c
+            copy_of(out_ref.at[block], block, flip_x, x0 + j).wait_send()
+            copy_of(out_ref.at[block], block, flip_c, c0 + j).wait_send()
+            copy_of(out_ref.at[other], other, flip_c, c0 + count + 1 + j).wait_send()
+
+        guarded(s, d, sent)
+    for s in (1, -1):
+        for d in range(0, zn - 1):
+            room = jnp.minimum(z - d, zn - 2 - z) if s == 1 else jnp.minimum(zn - 1 - d - z, z - 1)
+
+            @pl.when(room >= 0)
+            def _():
+                block = origin(s, d) + x * 2 + c
+                copy_of(out_ref.at[block], block, beside[s], slot_of[(s, d + 1)]).wait_send()
 
 
 def dft_even_odd(even_in, odd_in, use_cos):
@@ -175,39 +262,9 @@
     return out
 
 
-def estep_kernel(refs_ref, wt_ref, anorm_ref, prior_ref, hot_ref, pp_ref, ev_ref, mass_ref, cres, energy, bias, psum):
-    m_all = refs_ref.shape[0]
-    n = wt_ref.shape[1]
-    q = wt_ref.shape[2]
-    lane = lax.broadcasted_iota(jnp.int32, (n, q), 1)
-    sign = jnp.where(lane < R, jnp.float32(1.0), jnp.float32(-1.0))
-    energy[...] = jnp.zeros_like(energy)
-
-    def residue(r, count):
-        acc = None
-        sq = None
-        for t in range(count):
-            m = r + ROT * t
-            w = wt_ref[m]
-            turned = (pltpu.roll(w.astype(jnp.float32), R, 1) * sign).astype(jnp.bfloat16)
-            both = jnp.concatenate([w, turned], axis=0)
-            ref = refs_ref[m]
-            part = lax.dot_general(
-                both, ref, (((1,), (1,)), ((), ())), preferred_element_type=jnp.float32
-            )
-            acc = part if acc is None else acc + part
-            wide = ref.astype(jnp.float32)
-            sq = wide * wide if sq is None else sq + wide * wide
-        cres[r] = acc
-        energy[...] += sq
-
-    full, extra = m_all // ROT, m_all % ROT
-    if extra:
-        pl.loop(0, extra)(lambda r: residue(r, full + 1))
-    pl.loop(extra, ROT)(lambda r: residue(r, full))
-
+def scores_and_posterior(anorm, hot, prior_ref, pp_ref, ev_ref, mass_ref, cres, energy, bias, psum, evcol, n):
     norm = lax.dot_general(
-        anorm_ref[...], energy[...], (((1,), (1,)), ((), ())),
+        anorm, energy[...], (((1,), (1,)), ((), ())),
         preferred_element_type=jnp.float32, precision=HIGHEST,
     )
     bias[...] = jnp.log(prior_ref[...]) - norm
@@ -244,7 +301,7 @@
             expo[j] = jnp.exp(scores[j] - top)
             total = expo[j] if total is None else total + expo[j]
         norm_total = jnp.sum(total, axis=1, keepdims=True)
-        ev_ref[at, :] = jnp.broadcast_to(top + jnp.log(norm_total), (rows, 128))
+        evcol[at, :] = jnp.broadcast_to(top + jnp.log(norm_total), (rows, n))
         inv = 1.0 / norm_total
         psum[at, :] = total * inv
         u = {0: expo[0] * inv, HALF: expo[HALF] * inv}
@@ -258,8 +315,11 @@
             pp_ref[r, at, :] = real[r].astype(jnp.bfloat16)
             pp_ref[NC + r, at, :] = imag[r].astype(jnp.bfloat16)
 
+    square = (n, n)
+    eye = lax.broadcasted_iota(jnp.int32, square, 0) == lax.broadcasted_iota(jnp.int32, square, 1)
+    ev_ref[...] = jnp.sum(jnp.where(eye, evcol[...], 0.0), axis=0, keepdims=True)
     mass_ref[...] = lax.dot_general(
-        hot_ref[...], psum[...], (((1,), (0,)), ((), ())),
+        hot, psum[...], (((1,), (0,)), ((), ())),
         preferred_element_type=jnp.float32, precision=HIGHEST,
     )
 
@@ -391,44 +451,32 @@
 
     vmem = pl.BlockSpec(memory_space=pltpu.VMEM)
     hbm = pl.BlockSpec(memory_space=pl.ANY)
-    copies = 4 * zn - 1
     sem = pltpu.SemaphoreType.DMA
-    all_refs, wt, wpart, anorm, hot, table = pl.pallas_call(
+    copies = 8 * zn - 5
+    wt, wpart, table, pp, ev, mass = pl.pallas_call(
         functools.partial(gather_kernel, zn, dp, window),
         out_shape=(
-            jax.ShapeDtypeStruct((dp, mb, k, q), jnp.bfloat16),
             jax.ShapeDtypeStruct((m_all, n, q), jnp.bfloat16),
             jax.ShapeDtypeStruct((dp // 2, mb, n, q), jnp.bfloat16),
-            jax.ShapeDtypeStruct((n, q), jnp.float32),
-            jax.ShapeDtypeStruct((window, n), jnp.float32),
             jax.ShapeDtypeStruct((dp * window, q), jnp.float32),
+            jax.ShapeDtypeStruct((2 * NC, n, k), jnp.bfloat16),
+            jax.ShapeDtypeStruct((1, n), jnp.float32),
+            jax.ShapeDtypeStruct((window, k), jnp.float32),
         ),
         in_specs=[vmem] * 6,
-        out_specs=(hbm, vmem, hbm, vmem, vmem, vmem),
+        out_specs=(vmem, hbm, vmem, vmem, vmem, vmem),
         scratch_shapes=[
+            pltpu.VMEM((dp, mb, k, q), jnp.bfloat16),
+            pltpu.VMEM((ROT, 2 * n, k), jnp.float32),
+            pltpu.VMEM((k, q), jnp.float32),
+            pltpu.VMEM((n, k), jnp.float32),
+            pltpu.VMEM((n, k), jnp.float32),
+            pltpu.VMEM((n, n), jnp.float32),
             sem, sem((copies,)), sem((copies,)), sem((dp // 2,)), sem((dp // 2,)),
         ],
         compiler_params=pltpu.CompilerParams(collective_id=0, has_side_effects=True),
         name="gather",
-    )(refs, particles, ctf_group[:, None], ctf_group[None, :], defocus[:, None], cycle_weight[None, :])
-
-    pp, ev, mass = pl.pallas_call(
-        estep_kernel,
-        out_shape=(
-            jax.ShapeDtypeStruct((2 * NC, n, k), jnp.bfloat16),
-            jax.ShapeDtypeStruct((n, 128), jnp.float32),
-            jax.ShapeDtypeStruct((window, k), jnp.float32),
-        ),
-        in_specs=[vmem] * 5,
-        out_specs=(vmem,) * 3,
-        scratch_shapes=[
-            pltpu.VMEM((ROT, 2 * n, k), jnp.float32),
-            pltpu.VMEM((k, q), jnp.float32),
-            pltpu.VMEM((n, k), jnp.float32),
-            pltpu.VMEM((n, k), jnp.float32),
-        ],
-        name="estep",
-    )(all_refs.reshape(m_all, k, q), wt, anorm, class_prior[None, :], hot)
+    )(refs, particles, ctf_group[None, :], defocus[None, :], cycle_weight[None, :], class_prior[None, :])
 
     new_refs = pl.pallas_call(
         functools.partial(mstep_kernel, zn, dp),
@@ -450,7 +498,7 @@
         compiler_params=pltpu.CompilerParams(collective_id=1, has_side_effects=True),
         name="mstep",
     )(pp, wt, wpart, mass, table)
-    return (new_refs, ev[:, 0])
+    return (new_refs, ev[0])
 
 
 def solution(mesh):

time: 95.9 us -> 95.8 us (level)
  local copies, waits for them, and re-layouts: 5.19 us -> 2.39 us
  Pallas kernels: 89.8 us -> 92.6 us
    pallas_call x1, Pallas kernels: 36 us -> 52.9 us  [shards(): pl.pallas_call(functools.partial(gather_kernel, zn, dp, window), out_shap...]
    pallas_call x1 -> x0, Pallas kernels: 14.4 us -> none  [shards(): pl.pallas_call(estep_kernel, out_shape=(jax.ShapeDtypeStruct((2 * NC, n,...]
    broadcast_in_dim x2 -> x0, local copies, waits for them, and re-layouts: 2.69 us -> none  [the longest x1 1.36 us: shards(): ctf_group[:, None]]
    unnamed x3 -> x4, local copies, waits for them, and re-layouts: 1.87 us -> 2.39 us
where the time goes in v3:
time: 95.8 us; the launch traced here: 95.6 us
  Pallas kernels  92.6 us (97%)
  local copies, waits for them, and re-layouts  2.39 us (2%)
    pallas_call x1, Pallas kernels, shards(): pl.pallas_call(functools.partial(gather_kernel, zn, dp, window), out_shap...  52.9 us
    pallas_call x1, Pallas kernels, shards(): pl.pallas_call(functools.partial(mstep_kernel, zn, dp), out_shape=jax.Sha...  39.7 us
    unnamed x4, local copies, waits for them, and re-layouts  2.39 us

profile of v3, /device:TPU:0, one launch (start us, length us, event | category | flops | bytes accessed | tf_op | source)
XLA Modules:
  0.0 95.6 jit_solution(4617481235125399897)
XLA Ops:
  0.6 52.9 %gather.1 = (bf16[128,64,128]{2,1,0:T(8,128)(2,1)}, bf16[8,8,64,128]{3,2,1,0:T(8,128)(2,1)}, f32[128,128]{1,0:T(8,128)}, bf16[38,64,128]{2,1,0:T(8,128)(2,1)}, f32[1,64]{1,0:T(1,128)}, /*index=5*/f32[8,128]{1,0:T(8,128)}) custom-call(bf16[8,128,128]{2,1,0:T(8,128)(2,1)} %refs_ref.1, bf16[64,128,128]{2,1,0:T(8,128)(2,1)} %part_ref.1, s32[1,64]{1,0:T(1,128)} %bitcast.5, ...), custom_call_target="tpu_custom_call" | custom-call | tf_op jit(solution)/shard_map/gather/pallas_call | solution.py:456
  53.6 0.0 copy-start
  53.6 39.7 %mstep.1 = f32[8,128,128]{2,1,0:T(8,128)} custom-call(bf16[38,64,128]{2,1,0:T(8,128)(2,1)} %get-tuple-element.8.pp_ref, bf16[128,64,128]{2,1,0:T(8,128)(2,1)} %get-tuple-element.9.wt_ref, bf16[8,8,64,128]{3,2,1,0:T(8,128)(2,1)} %get-tuple-element.10.wpart_ref, f32[8,128]{1,0:T(8,128)} %get-tuple-element.11.mass_ref, f32[128,128]{1,0:T(8,128)} %get-tuple-element.12.table_ref), custom_call_target="tpu_custom_call" | custom-call | tf_op jit(solution)/shard_map/mstep/pallas_call | solution.py:481
  93.2 1.9 %copy.10 = f32[8,128,128]{2,1,0:T(8,128)} copy(f32[8,128,128]{2,1,0:T(8,128)} %mstep.1) | data formatting | bytes 1048576
  95.1 0.0 copy-done
  95.1 0.5 copy.11
Async XLA Ops:
  53.6 41.6 %copy-start = (f32[1,64]{1,0:T(1,128)S(1)}, f32[1,64]{1,0:T(1,128)}, u32[]{:S(2)}) copy-start(f32[1,64]{1,0:T(1,128)} %get-tuple-element.13) | copy-start | bytes 772

commit v4 on v3

--- a/solution.py
+++ b/solution.py
@@ -157,7 +157,25 @@
             energy[...] += wide * wide
 
     keep.wait()
-    products(me)
+    every = [(None, (1, 0))] + list(enumerate(steps))
+
+    def guarded(s, d, body):
+        if d == 0:
+            body()
+        else:
+            pl.when(holds(s, d))(body)
+
+    def from_x(j):
+        s, d = every[j][1]
+
+        def body():
+            block = origin(s, d) + (1 - x) * 2 + c
+            copy_of(out_ref.at[block], block, flip_x, x0 + j).wait_recv()
+            copy_of(out_ref.at[block], block, flip_c, c0 + count + 1 + j).start()
+            products(block)
+
+        guarded(s, d, body)
+
     for i, (s, d) in enumerate(steps):
         @pl.when(holds(s, d))
         def _():
@@ -169,37 +187,28 @@
                     copy_of(out_ref.at[block], block, beside[s], slot_of[(s, d + 1)]).start()
             copy_of(out_ref.at[block], block, flip_x, x0 + 1 + i).start()
             copy_of(out_ref.at[block], block, flip_c, c0 + 1 + i).start()
-            products(block)
-    every = [(None, (1, 0))] + list(enumerate(steps))
-
-    def guarded(s, d, body):
-        if d == 0:
-            body()
-        else:
-            pl.when(holds(s, d))(body)
-
-    for i, (s, d) in every:
-        j = 0 if i is None else i + 1
-
-        def from_x(s=s, d=d, j=j):
-            block = origin(s, d) + (1 - x) * 2 + c
-            copy_of(out_ref.at[block], block, flip_x, x0 + j).wait_recv()
-            copy_of(out_ref.at[block], block, flip_c, c0 + count + 1 + j).start()
-            products(block)
-            mine = origin(s, d) + x * 2 + (1 - c)
-            copy_of(out_ref.at[mine], mine, flip_c, c0 + j).wait_recv()
-            products(mine)
-
-        guarded(s, d, from_x)
-    for i, (s, d) in every:
-        j = 0 if i is None else i + 1
-
-        def from_core(s=s, d=d, j=j):
-            block = origin(s, d) + (1 - x) * 2 + (1 - c)
-            copy_of(out_ref.at[block], block, flip_c, c0 + count + 1 + j).wait_recv()
-            products(block)
-
-        guarded(s, d, from_core)
+            if i > 1:
+                products(block)
+        if i == 1:
+            products(me)
+            for late, (s1, d1) in enumerate(steps[:2]):
+                @pl.when(holds(s1, d1))
+                def _():
+                    products(origin(s1, d1) + x * 2 + c)
+        if i >= 1:
+            from_x(i - 1)
+    from_x(len(steps) - 1)
+    from_x(len(steps))
+    for half in (x, 1 - x):
+        for j, (_, (s, d)) in enumerate(every):
+            slot = c0 + j + (0 if half is x else count + 1)
+
+            def from_core(s=s, d=d, slot=slot, half=half):
+                block = origin(s, d) + half * 2 + (1 - c)
+                copy_of(out_ref.at[block], block, flip_c, slot).wait_recv()
+                products(block)
+
+            guarded(s, d, from_core)
 
     scores_and_posterior(anorm, hot, prior_ref, pp_ref, ev_ref, mass_ref, cres, energy, bias, psum, evcol, n)
 

time: 95.8 us -> 96.3 us (level)
  no operation moved by 1% of the time
where the time goes in v4:
time: 96.3 us; the launch traced here: 96.1 us
  Pallas kernels  93 us (97%)
  local copies, waits for them, and re-layouts  2.39 us (2%)
    pallas_call x1, Pallas kernels, shards(): pl.pallas_call(functools.partial(gather_kernel, zn, dp, window), out_shap...  53.4 us
    pallas_call x1, Pallas kernels, shards(): pl.pallas_call(functools.partial(mstep_kernel, zn, dp), out_shape=jax.Sha...  39.7 us
    unnamed x4, local copies, waits for them, and re-layouts  2.39 us

profile of v4, /device:TPU:0, one launch (start us, length us, event | category | flops | bytes accessed | tf_op | source)
XLA Modules:
  0.0 96.1 jit_solution(6444535182233374192)
XLA Ops:
  0.6 53.4 %gather.1 = (bf16[128,64,128]{2,1,0:T(8,128)(2,1)}, bf16[8,8,64,128]{3,2,1,0:T(8,128)(2,1)}, f32[128,128]{1,0:T(8,128)}, bf16[38,64,128]{2,1,0:T(8,128)(2,1)}, f32[1,64]{1,0:T(1,128)}, /*index=5*/f32[8,128]{1,0:T(8,128)}) custom-call(bf16[8,128,128]{2,1,0:T(8,128)(2,1)} %refs_ref.1, bf16[64,128,128]{2,1,0:T(8,128)(2,1)} %part_ref.1, s32[1,64]{1,0:T(1,128)} %bitcast.5, ...), custom_call_target="tpu_custom_call" | custom-call | tf_op jit(solution)/shard_map/gather/pallas_call | solution.py:465
  54.0 0.0 copy-start
  54.0 39.7 %mstep.1 = f32[8,128,128]{2,1,0:T(8,128)} custom-call(bf16[38,64,128]{2,1,0:T(8,128)(2,1)} %get-tuple-element.8.pp_ref, bf16[128,64,128]{2,1,0:T(8,128)(2,1)} %get-tuple-element.9.wt_ref, bf16[8,8,64,128]{3,2,1,0:T(8,128)(2,1)} %get-tuple-element.10.wpart_ref, f32[8,128]{1,0:T(8,128)} %get-tuple-element.11.mass_ref, f32[128,128]{1,0:T(8,128)} %get-tuple-element.12.table_ref), custom_call_target="tpu_custom_call" | custom-call | tf_op jit(solution)/shard_map/mstep/pallas_call | solution.py:490
  93.7 1.9 %copy.10 = f32[8,128,128]{2,1,0:T(8,128)} copy(f32[8,128,128]{2,1,0:T(8,128)} %mstep.1) | data formatting | bytes 1048576
  95.6 0.0 copy-done
  95.6 0.5 copy.11
Async XLA Ops:
  54.0 41.6 %copy-start = (f32[1,64]{1,0:T(1,128)S(1)}, f32[1,64]{1,0:T(1,128)}, u32[]{:S(2)}) copy-start(f32[1,64]{1,0:T(1,128)} %get-tuple-element.13) | copy-start | bytes 772
